TPU v7x, 512 devices: a whole 4x4x16 slice. The times are simulated.
512 devices in a mesh: dp: 8 (over y, core), expert: 64 (over x, z).
Axes of the slice: x: 4, y: 4, z: 16, core: 2. Of those that a mesh axis runs over, the one named last changes fastest.
Arguments:
- grad_out: bfloat16 [32768, 4096], P('expert', 'dp'), may hold values from -30 to 30
- hidden: bfloat16 [32768, 2, 1024], P('expert', None, 'dp'), may hold values from -24 to 24
- gate_prob: float32 [32768, 2], P('expert'), may hold values from 0.05 to 1
- expert_ids: int32 [32768, 2], P('expert'), may hold values from 0 to 63, all different within a row; in each aligned block of 512 rows (0 to 511, 512 to 1023, ...) at most 20 rows name the same one
- weights: bfloat16 [64, 1024, 4096], P('expert', None, 'dp'), may hold values from -0.1875 to 0.1875
Outputs:
- hidden_grad: bfloat16 [32768, 2, 1024], P('expert', None, 'dp')
- update: float32 [64, 1024, 4096], P('expert', None, 'dp')
Inputs may be any that keep to these rules, and one draw needn't show every extreme that they name: `expert_ids`: among the 512 tokens of one index of expert, no expert is named by more than 20 choices, a bound that some block reaches; the 2 experts of a token differ.
All inputs are finite; a program needn't handle non-finite values.
Results may differ from a plain program's by a relative error of at most 0.019.
Values may be sent and summed in bfloat16 or wider, within the bound.
No kernel may reach another device: no remote copies, remote signals or barrier semaphores. Data moves between devices by JAX's collectives and lax.ppermute only.
A program may use at most 64 MiB of HBM per device.

v0:
```python
import jax
import jax.numpy as jnp
from jax import lax
from jax.sharding import PartitionSpec as P

D = 4096


def slot_numbers(route_ids, capacity, expert_count):
    flat_ids = route_ids.reshape(-1)
    one_hot = (flat_ids[:, None] == jnp.arange(expert_count, dtype=jnp.int32)[None, :]).astype(
        jnp.int32
    )
    before = jnp.cumsum(one_hot, axis=0) - one_hot
    rank_in = jnp.sum(before * one_hot, axis=1)
    return flat_ids * capacity + rank_in


def gram_sum(matrix_part):
    partial_gram = jnp.dot(matrix_part, matrix_part.T, preferred_element_type=jnp.float32)
    return lax.psum(partial_gram.astype(jnp.bfloat16), "dp").astype(jnp.float32)


def place_slots(slot_index, values, slot_count):
    empty_rows = jnp.zeros((slot_count,) + values.shape[1:], values.dtype)
    return empty_rows.at[slot_index].set(values)


def per_device(grad_out, hidden, gate_prob, expert_ids, weights):
    tokens, width_part = grad_out.shape
    top_count = expert_ids.shape[1]
    experts = lax.axis_size("expert")
    capacity = 5 * tokens * top_count // (4 * experts)
    total_slots = experts * capacity
    pair_count = tokens * top_count
    slot_index = slot_numbers(expert_ids, capacity, experts)
    token_of = jnp.arange(pair_count, dtype=jnp.int32) // top_count
    send_grad = place_slots(slot_index, grad_out[token_of], total_slots).reshape(
        experts, capacity, width_part
    )
    scaled_part = (gate_prob[:, :, None] * hidden.astype(jnp.float32)).astype(jnp.bfloat16)
    whole_scaled = lax.all_gather(scaled_part, "dp", axis=2, tiled=True)
    send_scaled = place_slots(
        slot_index, whole_scaled.reshape(pair_count, -1), total_slots
    ).reshape(experts, capacity, -1)
    got_grad, got_scaled = (
        lax.all_to_all(send_grad, "expert", split_axis=0, concat_axis=0, tiled=True),
        lax.all_to_all(send_scaled, "expert", split_axis=0, concat_axis=0, tiled=True),
    )
    got_grad = got_grad.reshape(total_slots, width_part)
    got_scaled = got_scaled.reshape(total_slots, -1)
    weight_part = weights[0]
    gradient = lax.dot_general(
        got_scaled, got_grad, (((0,), (0,)), ((), ())), preferred_element_type=jnp.float32
    )
    back_term = lax.dot_general(
        got_grad, weight_part, (((1,), (1,)), ((), ())), preferred_element_type=jnp.float32
    )
    flat_prob = gate_prob.reshape(-1)
    summed = lax.psum_scatter(
        back_term.astype(jnp.bfloat16), "dp", scatter_dimension=1, tiled=True
    ).astype(jnp.float32)
    returned = lax.all_to_all(
        summed.reshape(experts, capacity, -1).astype(jnp.bfloat16),
        "expert",
        split_axis=0,
        concat_axis=0,
        tiled=True,
    ).astype(jnp.float32)
    picked = returned.reshape(total_slots, -1)[slot_index]
    hidden_grad = (flat_prob[:, None] * picked).astype(jnp.bfloat16).reshape(tokens, top_count, -1)
    grad_bf16 = gradient.astype(jnp.bfloat16)
    gram_first = gram_sum(grad_bf16)
    norm_sq = jnp.sqrt(jnp.sum(gram_first * gram_first)) + 1e-06
    current = (grad_bf16.astype(jnp.float32) * lax.rsqrt(norm_sq)).astype(jnp.bfloat16)
    gram_now = (gram_first / norm_sq).astype(jnp.bfloat16)
    following = current.astype(jnp.float32)
    for sweep_number in range(2):
        if sweep_number > 0:
            gram_now = gram_sum(current).astype(jnp.bfloat16)
        following = 1.5 * current.astype(jnp.float32) - 0.5 * jnp.dot(
            gram_now, current, preferred_element_type=jnp.float32
        )
        current = following.astype(jnp.bfloat16)
    update = following * D**0.5
    return (hidden_grad, update[None])


def solution(mesh):
    in_specs = (
        P("expert", "dp"),
        P("expert", None, "dp"),
        P("expert", None),
        P("expert", None),
        P("expert", None, "dp"),
    )
    out_specs = (P("expert", None, "dp"), P("expert", None, "dp"))
    return jax.shard_map(
        per_device, mesh=mesh, in_specs=in_specs, out_specs=out_specs, check_vma=False
    )
```

profile of v0, /device:TPU:2, one launch (start us, length us, event | category | flops | bytes accessed | tf_op | source)
XLA Modules:
  0.0 626.0 jit_solution(6197987789082699378)
XLA Ops:
  7.2 0.8 broadcast_multiply_fusion
  8.0 0.8 copy.19
  9.6 18.0 %reduce-window.6 = s32[64,8,128]{2,1,0:T(8,128)S(1)} reduce-window(s32[64,8,128]{2,1,0:T(8,128)S(1)} %fusion.21, s32[]{:T(128)} %constant.16.clone.1), window={size=1x1x128 pad=0_0x0_0x127_0}, to_apply=%region_0.0 | reduce-window | flops 8323072 | bytes 524292 | tf_op jit(solution)/shard_map/reduce-window
  28.2 12.8 %scatter_custom_fusion = bf16[1280,512]{1,0:T(8,128)(2,1)S(1)} fusion(s32[1024]{0:T(1024)S(1)} %bitcast.46, bf16[512,512]{1,0:T(8,128)(2,1)} %param.5, s32[1024]{0:T(1024)S(1)} %broadcast_clamp_fusion.1, bf16[]{:T(256)} %constant.13.clone.1), kind=kCustom, calls=%fused_computation.22 | custom fusion | bytes 1311232 | tf_op jit(solution)/shard_map/scatter | solution.py:26
  41.0 1.3 reshape.124
  42.3 94.8 %all_to_all.15 = bf16[64,20,512]{2,1,0:T(8,128)(2,1)S(1)} all-to-all(bf16[64,20,512]{2,1,0:T(8,128)(2,1)} %reshape.124), channel_id=1, replica_groups=mesh['dp'=8,'expert'=64] {'expert'}, dimensions={0} | all-to-all | bytes 2621440 | tf_op jit(solution)/shard_map/all_to_all | solution.py:47
  137.1 1.2 reshape.125
  138.3 4.4 convolution_convert_fusion
  142.7 4.4 copy.25
  147.1 35.3 %reduce-scatter.4.cloned.1.call-done = bf16[128,1280]{1,0:T(8,128)(2,1)} async-done(((bf16[1024,1280]{1,0:T(8,128)(2,1)}), bf16[128,1280]{1,0:T(8,128)(2,1)}) %reduce-scatter.4.cloned.1.call-update) | async-done | bytes 327696
  182.4 1.2 copy.26
  183.5 0.8 convert_element_type.61
  184.4 15.8 %all-to-all-start.1 = ((bf16[64,20,128]{2,1,0:T(8,128)(2,1)}), bf16[64,20,128]{2,1,0:T(8,128)(2,1)}, u32[]{:S(2)}, u32[]{:S(2)}) async-start(bf16[64,20,128]{2,1,0:T(8,128)(2,1)} %convert_element_type.61), calls=%async_computation.1 | async-start | bytes 786432 | tf_op jit(solution)/shard_map/all_to_all | solution.py:63
  200.4 23.1 %all-to-all-done.1 = bf16[64,20,128]{2,1,0:T(8,128)(2,1)} async-done(((bf16[64,20,128]{2,1,0:T(8,128)(2,1)}), bf16[64,20,128]{2,1,0:T(8,128)(2,1)}, u32[]{:S(2)}, u32[]{:S(2)}) %all-to-all-start.1) | async-done | bytes 327712 | tf_op jit(solution)/shard_map/all_to_all | solution.py:63
  223.6 1.1 reshape.131
  224.6 4.0 gather_fusion
  228.7 2.4 multiply_convert_fusion.2
  231.4 35.5 %all-gather.2.cloned.1.call-done = bf16[512,2,1024]{2,1,0:T(2,128)(2,1)} async-done(((bf16[512,2,128]{2,1,0:T(2,128)(2,1)}), bf16[512,2,1024]{2,1,0:T(2,128)(2,1)}) %all-gather.2.cloned.1.call-update) | async-done | bytes 2097168 | tf_op jit(solution)/shard_map/all_gather | solution.py:42
  266.8 4.1 reshape.160
  270.9 7.8 %scatter_custom_fusion.1 = bf16[1280,1024]{1,0:T(8,128)(2,1)} fusion(s32[1024]{0:T(1024)S(1)} %bitcast.48, bf16[1024,1024]{1,0:T(8,128)(2,1)} %reshape.160, bf16[]{:T(256)} %constant.13.clone.1), kind=kCustom, calls=%fused_computation.19 | custom fusion | bytes 2621952 | tf_op jit(solution)/shard_map/scatter | solution.py:26
  278.7 5.2 reshape.129
  283.9 159.6 %all_to_all.16 = bf16[64,20,1024]{2,1,0:T(8,128)(2,1)S(1)} all-to-all(bf16[64,20,1024]{2,1,0:T(8,128)(2,1)} %reshape.129), channel_id=1, replica_groups=mesh['dp'=8,'expert'=64] {'expert'}, dimensions={0} | all-to-all | bytes 5242880 | tf_op jit(solution)/shard_map/all_to_all | solution.py:48
  443.5 2.9 bitcast_convert_fusion
  446.4 1.0 copy-done.3
  447.3 2.6 convolution_convert_fusion.2
  450.2 73.4 %all-reduce.3.cloned.1.call-done = bf16[1024,1024]{1,0:T(8,128)(2,1)} async-done(((bf16[1024,1024]{1,0:T(8,128)(2,1)}), bf16[1024,1024]{1,0:T(8,128)(2,1)}) %all-reduce.3.cloned.1.call-update) | async-done | bytes 2097168 | tf_op jit(solution)/shard_map/psum | solution.py:21
  523.6 3.4 fusion
  527.8 2.9 subtract_convert_fusion
  530.8 1.0 copy-done.4
  531.7 2.6 convolution_convert_fusion.1
  534.4 80.9 %all-reduce.5.cloned.1.call-done = bf16[1024,1024]{1,0:T(8,128)(2,1)} async-done(((bf16[1024,1024]{1,0:T(8,128)(2,1)}), bf16[1024,1024]{1,0:T(8,128)(2,1)}) %all-reduce.5.cloned.1.call-update) | async-done | bytes 2097168 | tf_op jit(solution)/shard_map/psum | solution.py:21
  615.2 4.2 multiply_bitcast_fusion
  (35 shorter events, 2.1 us)
Async XLA Ops:
  7.2 131.1 %copy-start = (bf16[1,1024,512]{2,1,0:T(8,128)(2,1)S(1)}, bf16[1,1024,512]{2,1,0:T(8,128)(2,1)}, u32[]{:S(2)}) copy-start(bf16[1,1024,512]{2,1,0:T(8,128)(2,1)} %param.9) | copy-start | bytes 3145732
  7.2 175.2 %reduce-scatter.4.cloned.1.call-start = ((), (), s32[]{:S(2)}) async-start(), calls=%async_computation.7 | async-start | bytes 2949120
  147.1 53.2 %copy-start.2 = (f32[512,2]{0,1:T(2,128)S(1)}, f32[512,2]{0,1:T(2,128)}, u32[]{:S(2)}) copy-start(f32[512,2]{0,1:T(2,128)} %param.7) | copy-start | bytes 12292
  184.4 39.2 %all-to-all-start.1 = ((bf16[64,20,128]{2,1,0:T(8,128)(2,1)}), bf16[64,20,128]{2,1,0:T(8,128)(2,1)}, u32[]{:S(2)}, u32[]{:S(2)}) async-start(bf16[64,20,128]{2,1,0:T(8,128)(2,1)} %convert_element_type.61), calls=%async_computation.1 | async-start | bytes 786432 | tf_op jit(solution)/shard_map/all_to_all | solution.py:63
  200.2 66.6 %all-gather.2.cloned.1.call-start = ((), (), s32[]{:S(2)}) async-start(), calls=%async_computation.4 | async-start | bytes 2359296 | tf_op jit(solution)/shard_map/all_gather | solution.py:42
  231.1 292.5 %all-reduce.3.cloned.1.call-start = ((), (), s32[]{:S(2)}) async-start(), calls=%async_computation.5 | async-start | bytes 4194304 | tf_op jit(solution)/shard_map/psum | solution.py:21
  446.4 1.0 copy-start.3
  450.0 165.3 %all-reduce.5.cloned.1.call-start = ((), (), s32[]{:S(2)}) async-start(), calls=%async_computation.6 | async-start | bytes 4194304 | tf_op jit(solution)/shard_map/psum | solution.py:21
  523.6 4.2 copy-start.1
  530.8 1.0 copy-start.4
  534.3 80.9 %copy-start.5 = (bf16[1024,512]{1,0:T(8,128)(2,1)S(1)}, bf16[1024,512]{1,0:T(8,128)(2,1)}, u32[]{:S(2)}) copy-start(bf16[1024,512]{1,0:T(8,128)(2,1)} %copy-done.4) | copy-start | bytes 3145732
Sparse Core Ops, SparseCore 0:
  147.2 35.1 reduce-scatter.3
  231.2 35.5 all-gather.1
  450.1 73.4 all-reduce.2
  534.5 80.7 all-reduce.4
where the time goes:
time: 627 us; the launch traced here: 626 us
  blocking collectives  254 us (41%)
  waiting for transfers between devices  248 us (40%)
  local copies, waits for them, and re-layouts  47.8 us (8%)
  other arithmetic  24.9 us (4%)
  matrix products  19.6 us (3%)
  starting transfers between devices  16.4 us (3%)
  between operations  14.7 us (2%)
    all_to_all x1, blocking collectives, per_device(): lax.all_to_all(send_scaled, 'expert', split_axis=0, concat_axis=0, tiled=...  160 us
    psum x2, waiting for transfers between devices, gram_sum(): return lax.psum(partial_gram.astype(jnp.bfloat16), 'dp').astype(jnp.float32)  154 us
    all_to_all x1, blocking collectives, per_device(): lax.all_to_all(send_grad, 'expert', split_axis=0, concat_axis=0, tiled=True)  94.8 us
    all_gather x1, waiting for transfers between devices, per_device(): whole_scaled = lax.all_gather(scaled_part, 'dp', axis=2, tiled=True)  35.5 us
    unnamed x5, waiting for transfers between devices  35.4 us
    all_to_all x1, waiting for transfers between devices, per_device(): lax.all_to_all(summed.reshape(experts, capacity, -1).astype(jnp.bfloat16)...  23.1 us
    scatter x2, local copies, waits for them, and re-layouts, place_slots(): return empty_rows.at[slot_index].set(values)  20.6 us
    another operation x3, other arithmetic  18.2 us
  transfers between devices with their start and end apart: 5, of which 5 were waited for; matrix products, arithmetic and copies ran while one was open for 0% of the time, Pallas kernels for 0%

commit v1 on v0

--- a/solution.py
+++ b/solution.py
@@ -18,7 +18,9 @@
 
 def gram_sum(matrix_part):
     partial_gram = jnp.dot(matrix_part, matrix_part.T, preferred_element_type=jnp.float32)
-    return lax.psum(partial_gram.astype(jnp.bfloat16), "dp").astype(jnp.float32)
+    return jnp.sum(lax.all_gather(partial_gram.astype(jnp.bfloat16), "dp"), axis=0).astype(
+        jnp.float32
+    )
 
 
 def place_slots(slot_index, values, slot_count):

time: 627 us -> 664 us (1.059)
  the two profiles are of different devices: /device:TPU:2 before, /device:TPU:1 now
where the time goes in v1:
time: 664 us; the launch traced here: 663 us
  waiting for transfers between devices  284 us (43%)
  blocking collectives  246 us (37%)
  local copies, waits for them, and re-layouts  44.6 us (7%)
  other arithmetic  41.1 us (6%)
  matrix products  18.1 us (3%)
  starting transfers between devices  14.9 us (2%)
  between operations  14.7 us (2%)
    all_gather x2, waiting for transfers between devices, gram_sum(): lax.all_gather(partial_gram.astype(jnp.bfloat16), 'dp')  182 us
    all_to_all x1, blocking collectives, per_device(): lax.all_to_all(send_scaled, 'expert', split_axis=0, concat_axis=0, tiled=...  156 us
    all_to_all x1, blocking collectives, per_device(): lax.all_to_all(send_grad, 'expert', split_axis=0, concat_axis=0, tiled=True)  89.4 us
    all_gather x1, waiting for transfers between devices, per_device(): whole_scaled = lax.all_gather(scaled_part, 'dp', axis=2, tiled=True)  41.5 us
    unnamed x5, waiting for transfers between devices  39.7 us
    all_to_all x1, waiting for transfers between devices, per_device(): lax.all_to_all(summed.reshape(experts, capacity, -1).astype(jnp.bfloat16)...  20.8 us
    scatter x2, local copies, waits for them, and re-layouts, place_slots(): return empty_rows.at[slot_index].set(values)  20.6 us
    reduce_sum x2, other arithmetic, gram_sum(): jnp.sum(lax.all_gather(partial_gram.astype(jnp.bfloat16), 'dp'), axis=0)  18.9 us
  transfers between devices with their start and end apart: 5, of which 5 were waited for; matrix products, arithmetic and copies ran while one was open for 0% of the time, Pallas kernels for 0%

profile of v1, /device:TPU:1, one launch (start us, length us, event | category | flops | bytes accessed | tf_op | source)
XLA Modules:
  0.0 662.8 jit_solution(16515001811692064993)
XLA Ops:
  7.2 0.8 broadcast_multiply_fusion
  8.0 0.8 copy.27
  9.6 18.0 %reduce-window.6 = s32[64,8,128]{2,1,0:T(8,128)S(1)} reduce-window(s32[64,8,128]{2,1,0:T(8,128)S(1)} %fusion.21, s32[]{:T(128)} %constant.33.clone.1), window={size=1x1x128 pad=0_0x0_0x127_0}, to_apply=%region_0.0 | reduce-window | flops 8323072 | bytes 524292 | tf_op jit(solution)/shard_map/reduce-window
  28.2 12.8 %scatter_custom_fusion = bf16[1280,512]{1,0:T(8,128)(2,1)S(1)} fusion(s32[1024]{0:T(1024)S(1)} %bitcast.50, bf16[512,512]{1,0:T(8,128)(2,1)} %param.5, s32[1024]{0:T(1024)S(1)} %broadcast_clamp_fusion.1, bf16[]{:T(256)} %constant.16.clone.1), kind=kCustom, calls=%fused_computation.22 | custom fusion | bytes 1311232 | tf_op jit(solution)/shard_map/scatter | solution.py:28
  41.0 1.3 reshape.124
  42.3 89.4 %all_to_all.15 = bf16[64,20,512]{2,1,0:T(8,128)(2,1)S(1)} all-to-all(bf16[64,20,512]{2,1,0:T(8,128)(2,1)} %reshape.124), channel_id=1, replica_groups=mesh['dp'=8,'expert'=64] {'expert'}, dimensions={0} | all-to-all | bytes 2621440 | tf_op jit(solution)/shard_map/all_to_all | solution.py:49
  131.7 1.2 reshape.125
  132.9 4.4 convolution_convert_fusion
  137.3 4.4 copy.33
  141.7 39.6 %reduce-scatter.4.cloned.1.call-done = bf16[128,1280]{1,0:T(8,128)(2,1)} async-done(((bf16[1024,1280]{1,0:T(8,128)(2,1)}), bf16[128,1280]{1,0:T(8,128)(2,1)}) %reduce-scatter.4.cloned.1.call-update) | async-done | bytes 327696
  181.3 1.2 copy.34
  182.5 0.8 convert_element_type.65
  183.3 14.3 %all-to-all-start.1 = ((bf16[64,20,128]{2,1,0:T(8,128)(2,1)}), bf16[64,20,128]{2,1,0:T(8,128)(2,1)S(1)}, u32[]{:S(2)}, u32[]{:S(2)}) async-start(bf16[64,20,128]{2,1,0:T(8,128)(2,1)} %convert_element_type.65), calls=%async_computation.1 | async-start | bytes 786432 | tf_op jit(solution)/shard_map/all_to_all | solution.py:65
  197.8 20.8 %all-to-all-done.1 = bf16[64,20,128]{2,1,0:T(8,128)(2,1)S(1)} async-done(((bf16[64,20,128]{2,1,0:T(8,128)(2,1)}), bf16[64,20,128]{2,1,0:T(8,128)(2,1)S(1)}, u32[]{:S(2)}, u32[]{:S(2)}) %all-to-all-start.1) | async-done | bytes 327712 | tf_op jit(solution)/shard_map/all_to_all | solution.py:65
  218.7 2.8 gather_fusion
  221.5 1.4 multiply_convert_fusion.2
  223.2 41.5 %all-gather.6.cloned.1.call-done = bf16[512,2,1024]{2,1,0:T(2,128)(2,1)} async-done(((bf16[512,2,128]{2,1,0:T(2,128)(2,1)}), bf16[512,2,1024]{2,1,0:T(2,128)(2,1)}) %all-gather.6.cloned.1.call-update) | async-done | bytes 2097168 | tf_op jit(solution)/shard_map/all_gather | solution.py:44
  264.7 4.1 reshape.160
  268.8 7.8 %scatter_custom_fusion.1 = bf16[1280,1024]{1,0:T(8,128)(2,1)} fusion(s32[1024]{0:T(1024)S(1)} %bitcast.52, bf16[1024,1024]{1,0:T(8,128)(2,1)} %reshape.160, bf16[]{:T(256)} %constant.16.clone.1), kind=kCustom, calls=%fused_computation.19 | custom fusion | bytes 2621952 | tf_op jit(solution)/shard_map/scatter | solution.py:28
  276.6 5.2 reshape.129
  281.8 156.4 %all_to_all.16 = bf16[64,20,1024]{2,1,0:T(8,128)(2,1)S(1)} all-to-all(bf16[64,20,1024]{2,1,0:T(8,128)(2,1)} %reshape.129), channel_id=1, replica_groups=mesh['dp'=8,'expert'=64] {'expert'}, dimensions={0} | all-to-all | bytes 5242880 | tf_op jit(solution)/shard_map/all_to_all | solution.py:50
  438.2 2.9 bitcast_convert_fusion
  441.1 2.6 convolution_convert_fusion.2
  444.0 88.2 %all-gather.8.cloned.1.call-done = bf16[8192,1024]{1,0:T(8,128)(2,1)} async-done(((bf16[1024,1024]{1,0:T(8,128)(2,1)}), bf16[8192,1024]{1,0:T(8,128)(2,1)}) %all-gather.8.cloned.1.call-update) | async-done | bytes 16777232 | tf_op jit(solution)/shard_map/all_gather | solution.py:21
  532.2 9.5 %reduce_sum.46 = bf16[1024,1024]{1,0:T(8,128)(2,1)S(1)} reduce(bf16[8,1024,1024]{2,1,0:T(8,128)(2,1)} %bitcast.42, bf16[]{:T(256)} %constant.16.clone.1), dimensions={0}, to_apply=%region_6.7 | reduce | flops 7340032 | bytes 18874370 | tf_op jit(solution)/shard_map/reduce_sum | solution.py:21
  541.7 1.7 fusion
  544.1 1.4 subtract_convert_fusion
  545.5 1.0 copy-done.4
  546.5 2.6 convolution_convert_fusion.1
  549.1 93.5 %all-gather.10.cloned.1.call-done = bf16[8192,1024]{1,0:T(8,128)(2,1)} async-done(((bf16[1024,1024]{1,0:T(8,128)(2,1)}), bf16[8192,1024]{1,0:T(8,128)(2,1)}) %all-gather.10.cloned.1.call-update) | async-done | bytes 16777232 | tf_op jit(solution)/shard_map/all_gather | solution.py:21
  642.6 9.5 %reduce_sum.48 = bf16[1024,1024]{1,0:T(8,128)(2,1)S(1)} reduce(bf16[8,1024,1024]{2,1,0:T(8,128)(2,1)} %bitcast.43, bf16[]{:T(256)} %constant.16.clone.1), dimensions={0}, to_apply=%region_8.9 | reduce | flops 7340032 | bytes 18874370 | tf_op jit(solution)/shard_map/reduce_sum | solution.py:21
  652.0 4.2 multiply_bitcast_fusion
  (35 shorter events, 2.2 us)
Async XLA Ops:
  7.2 125.7 %copy-start = (bf16[1,1024,512]{2,1,0:T(8,128)(2,1)S(1)}, bf16[1,1024,512]{2,1,0:T(8,128)(2,1)}, u32[]{:S(2)}) copy-start(bf16[1,1024,512]{2,1,0:T(8,128)(2,1)} %param.9) | copy-start | bytes 3145732
  7.2 174.1 %reduce-scatter.4.cloned.1.call-start = ((), (), s32[]{:S(2)}) async-start(), calls=%async_computation.7 | async-start | bytes 2949120
  141.7 56.0 %copy-start.3 = (f32[512,2]{0,1:T(2,128)S(1)}, f32[512,2]{0,1:T(2,128)}, u32[]{:S(2)}) copy-start(f32[512,2]{0,1:T(2,128)} %param.7) | copy-start | bytes 12292
  183.3 35.3 %all-to-all-start.1 = ((bf16[64,20,128]{2,1,0:T(8,128)(2,1)}), bf16[64,20,128]{2,1,0:T(8,128)(2,1)S(1)}, u32[]{:S(2)}, u32[]{:S(2)}) async-start(bf16[64,20,128]{2,1,0:T(8,128)(2,1)} %convert_element_type.65), calls=%async_computation.1 | async-start | bytes 786432 | tf_op jit(solution)/shard_map/all_to_all | solution.py:65
  197.6 67.1 %all-gather.6.cloned.1.call-start = ((), (), s32[]{:S(2)}) async-start(), calls=%async_computation.4 | async-start | bytes 2359296 | tf_op jit(solution)/shard_map/all_gather | solution.py:44
  218.7 2.8 copy-start.2
  223.0 309.3 %all-gather.8.cloned.1.call-start = ((), (), s32[]{:S(2)}) async-start(), calls=%async_computation.5 | async-start | bytes 18874368 | tf_op jit(solution)/shard_map/all_gather | solution.py:21
  443.7 198.9 %all-gather.10.cloned.1.call-start = ((), (), s32[]{:S(2)}) async-start(), calls=%async_computation.6 | async-start | bytes 18874368 | tf_op jit(solution)/shard_map/all_gather | solution.py:21
  545.5 1.0 copy-start.4
  652.0 4.3 copy-start.1
Sparse Core Ops, SparseCore 0:
  141.8 39.4 reduce-scatter.3
  223.1 41.6 all-gather.5
  443.8 88.3 all-gather.7
  549.2 93.2 all-gather.9
